TPU v7x, 32 devices: a whole 2x2x4 slice. The times are simulated.
32 devices in a mesh: dp: 2 (over x), ts: 16 (over z, y, core).
Axes of the slice: x: 2, y: 2, z: 4, core: 2. Of those that a mesh axis runs over, the one named last changes fastest.
Arguments:
- clip_video: bfloat16 [64, 4, 40, 128], P(('dp', 'ts')), may hold values from -6 to 6
- conv_weight: bfloat16 [3, 3, 3, 128, 128], replicated, may hold values from -0.109375 to 0.109375
- embed_weight: bfloat16 [128, 5120], replicated, may hold values from -0.5 to 0.5
- gain_spatial: float32 [5120], replicated, may hold values from 0.5 to 1.5
- gain_temporal: float32 [5120], replicated, may hold values from 0.5 to 1.5
- input_spatial: bfloat16 [5120, 384], P(('dp', 'ts')), may hold values from -0.078125 to 0.078125
- input_temporal: bfloat16 [5120, 384], P(('dp', 'ts')), may hold values from -0.078125 to 0.078125
- output_spatial: bfloat16 [128, 5120], replicated, may hold values from -2 to 2
- output_temporal: bfloat16 [128, 5120], replicated, may hold values from -2 to 2
- cotangent: bfloat16 [64, 4, 40, 5120], P(('dp', 'ts')), may hold values from -6 to 6
Outputs:
- layer_output: bfloat16 [64, 4, 40, 5120], P(('dp', 'ts'))
- grad_spatial: float32 [5120, 384], P(('dp', 'ts'))
All inputs are finite; a program needn't handle non-finite values.
Results may differ from a plain program's by a relative error of at most 0.015.
Values may be sent and summed in bfloat16 or wider, within the bound.
A program may use at most 128 MiB of HBM per device.

v0:
```python
import jax
import jax.numpy as jnp
from jax import lax
from jax.sharding import PartitionSpec as P

FR = 16
epsilon = 1e-06
masked = -1e30
F32 = jnp.float32
BF16 = jnp.bfloat16


def mm(a, b, dims=((1,), (0,))):
    return lax.dot_general(a, b, (dims, ((), ())), preferred_element_type=F32)


def mm_t(a, b):
    return mm(a, b, ((1,), (1,)))


def t_mm(a, b):
    return mm(a, b, ((0,), (0,)))


def wide_mm(a, b):
    high = b.astype(BF16)
    low = (b - high.astype(F32)).astype(BF16)
    return mm(a, high) + mm(a, low)


def conv_local(volume, weight, count):
    frames, height, columns, channels = volume.shape
    padded = jnp.pad(volume, ((0, 0), (1, 1), (1, 1), (0, 0)))
    summed = jnp.zeros((count * height * columns, weight.shape[-1]), F32)
    for a in range(3):
        for b in range(3):
            for e in range(3):
                window = padded[2 - a : 2 - a + count, b : b + height, e : e + columns, :]
                summed = summed + mm(window.reshape(-1, channels), weight[a, b, e])
    return summed


def attend_forward(q, k, v, allowed):
    scores = mm_t(q, k) * q.shape[-1] ** (-0.5)
    scores = jnp.where(allowed, scores, masked)
    raised = jnp.exp(scores - jnp.max(scores, axis=-1, keepdims=True))
    attend = raised / jnp.sum(raised, axis=-1, keepdims=True)
    return (mm(attend.astype(BF16), v).astype(BF16), attend)


def attend_backward(q, k, v, attend, g):
    scale = q.shape[-1] ** (-0.5)
    grad_attend = mm_t(g, v)
    grad_values = t_mm(attend.astype(BF16), g)
    inner = jnp.sum(grad_attend * attend, axis=-1, keepdims=True)
    grad_scores = (attend * (grad_attend - inner)).astype(BF16)
    grad_q = mm(grad_scores, k) * scale
    grad_k = t_mm(grad_scores, q) * scale
    return jnp.concatenate([grad_q, grad_k, grad_values], axis=-1).astype(BF16)


def shards(
    clip_video,
    conv_weight,
    embed_weight,
    gain_spatial,
    gain_temporal,
    input_spatial,
    input_temporal,
    output_spatial,
    output_temporal,
    cotangent,
):
    frames, height, columns, channels = clip_video.shape
    rows, triple = input_spatial.shape
    head = triple // 3
    width = embed_weight.shape[-1]
    places = height * columns
    tokens = frames * places
    ts = lax.axis_size("ts")
    team = FR // frames
    share = places // team
    groups = [[c * team + i for i in range(team)] for c in range(ts // team)]
    me = lax.axis_index("dp") * ts + lax.axis_index("ts")
    route = [(i - 1, i) for i in range(1, ts)]
    prior = lax.ppermute(clip_video, "ts", route)
    volume = jnp.concatenate([prior, clip_video], axis=0)
    basis = jnp.concatenate([embed_weight, output_spatial], axis=0)
    window = lax.dynamic_slice(basis, (0, me * rows), (basis.shape[0], rows)).astype(F32)
    gain_s = lax.dynamic_slice(gain_spatial, (me * rows,), (rows,))
    gain_t = lax.dynamic_slice(gain_temporal, (me * rows,), (rows,))
    embed_rows = (window[:channels] * gain_s).astype(BF16)
    part = jnp.concatenate(
        [mm(embed_rows, input_spatial), mm((window * gain_t).astype(BF16), input_temporal)], axis=0
    )
    mixed = lax.psum(part.astype(BF16), ("dp", "ts"))
    map_space, map_time = (mixed[:channels], mixed[channels:])
    gram = mm_t(basis, basis)
    cotangent_rows = cotangent.reshape(tokens, width)
    grad_mix_time = mm_t(cotangent_rows, output_temporal).astype(BF16)
    grad_direct = mm_t(cotangent_rows, output_spatial)
    features = jax.nn.gelu(conv_local(volume, conv_weight, frames), approximate=True).astype(BF16)
    squares = jnp.sum(
        wide_mm(features, gram[:channels, :channels]) * features.astype(F32), axis=-1, keepdims=True
    )
    factor_one = lax.rsqrt(jnp.maximum(squares, 0.0) / width + epsilon)
    packed_one = (mm(features, map_space) * factor_one).astype(BF16)
    place = jnp.arange(tokens)
    same_frame = place[:, None] // places == place[None, :] // places
    q, k, v = (packed_one[:, :head], packed_one[:, head : 2 * head], packed_one[:, 2 * head :])
    mixture_one, attend_one = attend_forward(q, k, v, same_frame)
    joint = jnp.concatenate([features, mixture_one], axis=-1)
    spread = wide_mm(joint, gram)
    squares = jnp.sum(spread * joint.astype(F32), axis=-1, keepdims=True)
    factor_two = lax.rsqrt(jnp.maximum(squares, 0.0) / width + epsilon)
    packed_two = (mm(joint, map_time) * factor_two).astype(BF16)
    sent = jnp.concatenate([packed_two, grad_mix_time], axis=-1).reshape(frames, places, 4 * head)
    got = lax.all_to_all(
        sent, "ts", split_axis=1, concat_axis=0, tiled=True, axis_index_groups=groups
    ).reshape(FR * share, 4 * head)
    spot = jnp.arange(FR * share)
    allowed = (spot[:, None] % share == spot[None, :] % share) & (spot[:, None] >= spot[None, :])
    tq, tk, tv, tg = (got[:, i * head : (i + 1) * head] for i in range(4))
    mixture_two, attend_two = attend_forward(tq, tk, tv, allowed)
    grad_two = attend_backward(tq, tk, tv, attend_two, tg)
    back = jnp.concatenate([mixture_two, grad_two], axis=-1).reshape(FR, share, 4 * head)
    home = lax.all_to_all(
        back, "ts", split_axis=0, concat_axis=1, tiled=True, axis_index_groups=groups
    ).reshape(tokens, 4 * head)
    mixture_two, grad_two = (home[:, :head], home[:, head:])
    output = mm(
        jnp.concatenate([joint, mixture_two], axis=-1),
        jnp.concatenate([basis, output_temporal], axis=0),
    ).astype(BF16)
    inner = jnp.sum(grad_two.astype(F32) * packed_two.astype(F32), axis=-1, keepdims=True)
    grad_mix_one = (
        grad_direct
        + factor_two * mm_t(grad_two, map_time[channels:])
        - factor_two**2 * inner / width * spread[:, channels:]
    ).astype(BF16)
    grad_one = attend_backward(q, k, v, attend_one, grad_mix_one)
    scaled = (features.astype(F32) * factor_one).astype(BF16)
    core = lax.psum(t_mm(scaled, grad_one).astype(BF16), ("dp", "ts"))
    return (output.reshape(frames, height, columns, width), t_mm(embed_rows, core))


def solution(mesh):
    placed = (
        P(("dp", "ts"), None, None, None),
        P(),
        P(),
        P(),
        P(),
        P(("dp", "ts"), None),
        P(("dp", "ts"), None),
        P(),
        P(),
        P(("dp", "ts"), None, None, None),
    )
    return jax.shard_map(
        shards,
        mesh=mesh,
        in_specs=placed,
        out_specs=(P(("dp", "ts"), None, None, None), P(("dp", "ts"), None)),
        check_vma=False,
    )
```

profile of v0, /device:TPU:8, one launch (start us, length us, event | category | flops | bytes accessed | tf_op | source)
XLA Modules:
  0.0 330.4 jit_solution(1640951019662262618)
XLA Ops:
  7.2 2.2 collective-permute-start
  9.4 2.5 constant_dynamic-update-slice_fusion.3
  11.9 2.5 constant_dynamic-update-slice_fusion.2
  17.0 1.2 convolution_convert_fusion.1
  18.2 1.1 convolution_convert_fusion.3
  20.1 3.5 %fusion.148 = f32[256,256]{1,0:T(8,128)S(1)} fusion(bf16[256,5120]{1,0:T(8,128)(2,1)} %constant_dynamic-update-slice_fusion.2), kind=kOutput, calls=%fused_computation.247 | convolution fusion | flops 671088640 | bytes 2883584 | tf_op jit(solution)/shard_map/dot_general | solution.py:14
  30.7 120.0 %all-reduce.4.cloned.1.call-done = bf16[384,384]{1,0:T(8,128)(2,1)} async-done(((bf16[384,384]{1,0:T(8,128)(2,1)}), bf16[384,384]{1,0:T(8,128)(2,1)}) %all-reduce.4.cloned.1.call-update) | async-done | bytes 294928 | tf_op jit(solution)/shard_map/psum | solution.py:96
  150.8 1.1 fusion.7
  155.4 1.0 copy.12
  156.5 4.2 %all-to-all-start = ((bf16[2,160,512]{2,0,1:T(2,128)(2,1)}), bf16[2,160,512]{2,0,1:T(2,128)(2,1)}, u32[]{:S(2)}, u32[]{:S(2)}) async-start(bf16[2,160,512]{2,0,1:T(2,128)(2,1)} %copy.12), calls=%async_computation | async-start | bytes 655360 | tf_op jit(solution)/shard_map/all_to_all | solution.py:118
  160.7 6.2 %all-to-all-done = bf16[2,160,512]{2,0,1:T(2,128)(2,1)} async-done(((bf16[2,160,512]{2,0,1:T(2,128)(2,1)}), bf16[2,160,512]{2,0,1:T(2,128)(2,1)}, u32[]{:S(2)}, u32[]{:S(2)}) %all-to-all-start) | async-done | bytes 327712 | tf_op jit(solution)/shard_map/all_to_all | solution.py:118
  166.9 1.8 copy.13
  168.7 1.8 reshape.248
  170.5 1.2 fusion.147
  171.8 1.2 convolution_convert_fusion.7
  174.9 1.8 reshape.249
  176.7 10.8 %all_to_all.30 = bf16[16,20,512]{2,1,0:T(8,128)(2,1)S(1)} all-to-all(bf16[16,20,512]{2,1,0:T(8,128)(2,1)} %reshape.249), channel_id=1, replica_groups={{0,1,2,3,4,5,6,7},{8,9,10,11,12,13,14,15},{16,17,18,19,20,21,22,23},{24..., dimensions={0} | all-to-all | bytes 655360 | tf_op jit(solution)/shard_map/all_to_all | solution.py:127
  188.7 1.8 reshape.250
  190.5 1.2 multiply_reduce_fusion.1
  191.7 1.3 convolution_multiply_fusion.6
  193.0 2.4 fusion.16
  197.7 5.7 %convolution_convert_fusion = bf16[320,5120]{1,0:T(8,128)(2,1)} fusion(bf16[128,5120]{1,0:T(8,128)(2,1)} %param.18, bf16[128,5120]{1,0:T(8,128)(2,1)} %param.17, bf16[128,5120]{1,0:T(8,128)(2,1)} %param.12, bf16[320,128]{1,0:T(8,128)(2,1)S(1)} %slice-done, bf16[320,128]{1,0:T(8,128)(2,1)S(1)} %convolution_convert_fusion.8, bf16[320,128]{1,0:T(8,128)(2,1)S(1)} %fusion.43), kind=kOutput, calls=%fused_computation | convolution fusion | flops 1272463360 | bytes 7454720 | tf_op jit(solution)/shard_map/dot_general | solution.py:14
  203.3 118.4 %all-reduce.6.cloned.1.call-done = bf16[128,384]{1,0:T(8,128)(2,1)} async-done(((bf16[128,384]{1,0:T(8,128)(2,1)}), bf16[128,384]{1,0:T(8,128)(2,1)}) %all-reduce.6.cloned.1.call-update) | async-done | bytes 98320 | tf_op jit(solution)/shard_map/psum | solution.py:143
  321.7 1.9 fusion.129
  (102 shorter events, 19.2 us)
Async XLA Ops:
  7.2 16.5 %copy-start = (bf16[2,4,40,5120]{3,2,1,0:T(8,128)(2,1)S(1)}, bf16[2,4,40,5120]{3,2,1,0:T(8,128)(2,1)}, u32[]{:S(2)}) copy-start(bf16[2,4,40,5120]{3,2,1,0:T(8,128)(2,1)} %param.19) | copy-start | bytes 9830404
  7.2 143.6 %all-reduce.4.cloned.1.call-start = ((), (), s32[]{:S(2)}) async-start(), calls=%async_computation.2 | async-start | bytes 589824 | tf_op jit(solution)/shard_map/psum | solution.py:96
  7.2 17.5 %collective-permute-start = (bf16[2,4,40,128]{3,2,1,0:T(8,128)(2,1)}, bf16[2,4,40,128]{3,2,1,0:T(8,128)(2,1)S(1)}, u32[]{:S(2)}, u32[]{:S(2)}) collective-permute-start(bf16[2,4,40,128]{3,2,1,0:T(8,128)(2,1)} %param.10), channel_id=1, source_target_pairs={{0,1},{1,2},{2,3},{3,4},{4,5},{5,6},{6,7},{7,8},{8,9},{9,10},{10,1... | collective-permute-start | bytes 245768 | tf_op jit(solution)/shard_map/ppermute | solution.py:86
  9.4 7.6 %copy-start.13 = (bf16[160,384]{1,0:T(8,128)(2,1)S(1)}, bf16[160,384]{1,0:T(8,128)(2,1)}, u32[]{:S(2)}) copy-start(bf16[160,384]{1,0:T(8,128)(2,1)} %param.16) | copy-start | bytes 368644
  15.4 2.8 copy-start.6
  20.1 3.6 %copy-start.5 = (bf16[128,5120]{1,0:T(8,128)(2,1)S(1)}, bf16[128,5120]{1,0:T(8,128)(2,1)}, u32[]{:S(2)}) copy-start(bf16[128,5120]{1,0:T(8,128)(2,1)} %param.18) | copy-start | bytes 3932164
  23.6 6.8 %copy-start.3 = (f32[256,256]{1,0:T(8,128)}, f32[256,256]{1,0:T(8,128)S(1)}, u32[]{:S(2)}) copy-start(f32[256,256]{1,0:T(8,128)S(1)} %fusion.148) | copy-start | bytes 786436
  23.7 1.1 copy-start.12
  24.7 1.2 copy-start.8
  150.7 2.5 copy-start.4
  151.9 1.3 copy-start.10
  151.9 2.5 copy-start.14
  152.2 0.8 copy-start.1
  154.7 0.7 copy-start.7
  156.5 10.4 %all-to-all-start = ((bf16[2,160,512]{2,0,1:T(2,128)(2,1)}), bf16[2,160,512]{2,0,1:T(2,128)(2,1)}, u32[]{:S(2)}, u32[]{:S(2)}) async-start(bf16[2,160,512]{2,0,1:T(2,128)(2,1)} %copy.12), calls=%async_computation | async-start | bytes 655360 | tf_op jit(solution)/shard_map/all_to_all | solution.py:118
  160.7 161.0 %all-reduce.6.cloned.1.call-start = ((), (), s32[]{:S(2)}) async-start(), calls=%async_computation.3 | async-start | bytes 196608 | tf_op jit(solution)/shard_map/psum | solution.py:143
  170.5 2.5 copy-start.9
  193.0 2.4 copy-start.2
  193.0 2.4 copy-start.11
  195.7 1.9 slice-start
Sparse Core Ops, SparseCore 0:
  20.2 130.4 all-reduce.3
  197.8 123.8 all-reduce.5
where the time goes:
time: 331 us; the launch traced here: 330 us
  waiting for transfers between devices  245 us (74%)
  matrix products  31.3 us (9%)
  local copies, waits for them, and re-layouts  18.4 us (6%)
  between operations  14.5 us (4%)
  blocking collectives  10.8 us (3%)
  starting transfers between devices  6.42 us (2%)
  other arithmetic  4.29 us (1%)
    psum x1, waiting for transfers between devices, shards(): mixed = lax.psum(part.astype(BF16), ('dp', 'ts'))  120 us
    psum x1, waiting for transfers between devices, shards(): core = lax.psum(t_mm(scaled, grad_one).astype(BF16), ('dp', 'ts'))  118 us
    dot_general x54, matrix products, mm(): return lax.dot_general(a, b, (dims, ((), ())), preferred_element_type=F32)  31.3 us
    all_to_all x1, blocking collectives, shards(): lax.all_to_all(back, 'ts', split_axis=0, concat_axis=1, tiled=True, axis_...  10.8 us
  transfers between devices with their start and end apart: 4, of which 3 were waited for; matrix products, arithmetic and copies ran while one was open for 8% of the time, Pallas kernels for 0%

commit v1 on v0

--- a/solution.py
+++ b/solution.py
@@ -93,7 +93,7 @@
     part = jnp.concatenate(
         [mm(embed_rows, input_spatial), mm((window * gain_t).astype(BF16), input_temporal)], axis=0
     )
-    mixed = lax.psum(part.astype(BF16), ("dp", "ts"))
+    mixed = lax.psum(lax.psum(part.astype(BF16), "ts"), "dp")
     map_space, map_time = (mixed[:channels], mixed[channels:])
     gram = mm_t(basis, basis)
     cotangent_rows = cotangent.reshape(tokens, width)

time: 331 us -> 318 us (0.961)
  waiting for transfers between devices: 245 us -> 230 us
    psum x1 -> x2, waiting for transfers between devices: 120 us -> 106 us  [shards(): mixed = lax.psum(lax.psum(part.astype(BF16), 'ts'), 'dp')]
  transfers between devices with their start and end apart: 4 -> 5, of which waited for: 3 -> 4; matrix products, arithmetic and copies ran while one was open for 8% -> 9% of each run, Pallas kernels for 0% -> 0%
where the time goes in v1:
time: 318 us; the launch traced here: 317 us
  waiting for transfers between devices  230 us (72%)
  matrix products  32.7 us (10%)
  local copies, waits for them, and re-layouts  18.5 us (6%)
  between operations  14.2 us (4%)
  blocking collectives  10.8 us (3%)
  starting transfers between devices  6.78 us (2%)
  other arithmetic  4.29 us (1%)
    psum x1, waiting for transfers between devices, shards(): core = lax.psum(t_mm(scaled, grad_one).astype(BF16), ('dp', 'ts'))  118 us
    psum x2, waiting for transfers between devices, shards(): mixed = lax.psum(lax.psum(part.astype(BF16), 'ts'), 'dp')  106 us
    dot_general x54, matrix products, mm(): return lax.dot_general(a, b, (dims, ((), ())), preferred_element_type=F32)  32.7 us
    all_to_all x1, blocking collectives, shards(): lax.all_to_all(back, 'ts', split_axis=0, concat_axis=1, tiled=True, axis_...  10.8 us
  transfers between devices with their start and end apart: 5, of which 4 were waited for; matrix products, arithmetic and copies ran while one was open for 9% of the time, Pallas kernels for 0%

profile of v1, /device:TPU:8, one launch (start us, length us, event | category | flops | bytes accessed | tf_op | source)
XLA Modules:
  0.0 317.3 jit_solution(11479207326354246197)
XLA Ops:
  7.2 2.2 collective-permute-start
  9.4 2.5 constant_dynamic-update-slice_fusion.3
  11.9 2.5 constant_dynamic-update-slice_fusion.2
  17.0 1.2 convolution_convert_fusion.1
  20.2 3.5 %fusion.148 = f32[256,256]{1,0:T(8,128)S(1)} fusion(bf16[256,5120]{1,0:T(8,128)(2,1)} %constant_dynamic-update-slice_fusion.2), kind=kOutput, calls=%fused_computation.247 | convolution fusion | flops 671088640 | bytes 2883584 | tf_op jit(solution)/shard_map/dot_general | solution.py:14
  23.7 1.6 convolution_convert_fusion.4
  31.1 81.8 %all-reduce.5.cloned.1.call-done = bf16[384,384]{1,0:T(8,128)(2,1)} async-done(((bf16[384,384]{1,0:T(8,128)(2,1)}), bf16[384,384]{1,0:T(8,128)(2,1)}) %all-reduce.5.cloned.1.call-update) | async-done | bytes 294928 | tf_op jit(solution)/shard_map/psum | solution.py:96
  114.0 23.9 %all-reduce.7.cloned.1.call-done = bf16[384,384]{1,0:T(8,128)(2,1)} async-done(((bf16[384,384]{1,0:T(8,128)(2,1)}), bf16[384,384]{1,0:T(8,128)(2,1)}) %all-reduce.7.cloned.1.call-update) | async-done | bytes 294928 | tf_op jit(solution)/shard_map/psum | solution.py:96
  138.0 1.1 fusion.7
  143.7 4.5 %all-to-all-start = ((bf16[2,160,512]{2,0,1:T(2,128)(2,1)}), bf16[2,160,512]{2,0,1:T(2,128)(2,1)}, u32[]{:S(2)}, u32[]{:S(2)}) async-start(bf16[2,160,512]{2,0,1:T(2,128)(2,1)} %copy.12), calls=%async_computation | async-start | bytes 655360 | tf_op jit(solution)/shard_map/all_to_all | solution.py:118
  148.2 6.3 %all-to-all-done = bf16[2,160,512]{2,0,1:T(2,128)(2,1)} async-done(((bf16[2,160,512]{2,0,1:T(2,128)(2,1)}), bf16[2,160,512]{2,0,1:T(2,128)(2,1)}, u32[]{:S(2)}, u32[]{:S(2)}) %all-to-all-start) | async-done | bytes 327712 | tf_op jit(solution)/shard_map/all_to_all | solution.py:118
  154.5 1.8 copy.13
  156.2 1.8 reshape.248
  158.0 1.2 fusion.147
  159.4 1.2 convolution_convert_fusion.7
  162.5 1.8 reshape.249
  164.2 10.8 %all_to_all.30 = bf16[16,20,512]{2,1,0:T(8,128)(2,1)S(1)} all-to-all(bf16[16,20,512]{2,1,0:T(8,128)(2,1)} %reshape.249), channel_id=1, replica_groups={{0,1,2,3,4,5,6,7},{8,9,10,11,12,13,14,15},{16,17,18,19,20,21,22,23},{24..., dimensions={0} | all-to-all | bytes 655360 | tf_op jit(solution)/shard_map/all_to_all | solution.py:127
  176.3 1.8 reshape.250
  178.1 1.2 multiply_reduce_fusion.1
  179.3 1.3 convolution_multiply_fusion.6
  180.6 2.4 fusion.16
  185.2 5.7 %convolution_convert_fusion = bf16[320,5120]{1,0:T(8,128)(2,1)} fusion(bf16[128,5120]{1,0:T(8,128)(2,1)} %param.18, bf16[128,5120]{1,0:T(8,128)(2,1)} %param.17, bf16[128,5120]{1,0:T(8,128)(2,1)} %param.12, bf16[320,128]{1,0:T(8,128)(2,1)S(1)} %slice-done, bf16[320,128]{1,0:T(8,128)(2,1)S(1)} %convolution_convert_fusion.8, bf16[320,128]{1,0:T(8,128)(2,1)S(1)} %fusion.43), kind=kOutput, calls=%fused_computation | convolution fusion | flops 1272463360 | bytes 7454720 | tf_op jit(solution)/shard_map/dot_general | solution.py:14
  190.9 118.0 %all-reduce.9.cloned.1.call-done = bf16[128,384]{1,0:T(8,128)(2,1)} async-done(((bf16[128,384]{1,0:T(8,128)(2,1)}), bf16[128,384]{1,0:T(8,128)(2,1)}) %all-reduce.9.cloned.1.call-update) | async-done | bytes 98320 | tf_op jit(solution)/shard_map/psum | solution.py:143
  308.9 1.9 fusion.129
  (107 shorter events, 21.2 us)
Async XLA Ops:
  7.2 16.5 %copy-start = (bf16[2,4,40,5120]{3,2,1,0:T(8,128)(2,1)S(1)}, bf16[2,4,40,5120]{3,2,1,0:T(8,128)(2,1)}, u32[]{:S(2)}) copy-start(bf16[2,4,40,5120]{3,2,1,0:T(8,128)(2,1)} %param.19) | copy-start | bytes 9830404
  7.2 105.7 %all-reduce.5.cloned.1.call-start = ((), (), s32[]{:S(2)}) async-start(), calls=%async_computation.2 | async-start | bytes 589824 | tf_op jit(solution)/shard_map/psum | solution.py:96
  7.2 18.1 %collective-permute-start = (bf16[2,4,40,128]{3,2,1,0:T(8,128)(2,1)}, bf16[2,4,40,128]{3,2,1,0:T(8,128)(2,1)S(1)}, u32[]{:S(2)}, u32[]{:S(2)}) collective-permute-start(bf16[2,4,40,128]{3,2,1,0:T(8,128)(2,1)} %param.10), channel_id=1, source_target_pairs={{0,1},{1,2},{2,3},{3,4},{4,5},{5,6},{6,7},{7,8},{8,9},{9,10},{10,1... | collective-permute-start | bytes 245768 | tf_op jit(solution)/shard_map/ppermute | solution.py:86
  9.4 7.6 %copy-start.14 = (bf16[160,384]{1,0:T(8,128)(2,1)S(1)}, bf16[160,384]{1,0:T(8,128)(2,1)}, u32[]{:S(2)}) copy-start(bf16[160,384]{1,0:T(8,128)(2,1)} %param.16) | copy-start | bytes 368644
  15.4 2.8 copy-start.6
  20.1 117.9 %all-reduce.7.cloned.1.call-start = ((), (), s32[]{:S(2)}) async-start(), calls=%async_computation.3 | async-start | bytes 589824 | tf_op jit(solution)/shard_map/psum | solution.py:96
  20.1 3.6 %copy-start.5 = (bf16[128,5120]{1,0:T(8,128)(2,1)S(1)}, bf16[128,5120]{1,0:T(8,128)(2,1)}, u32[]{:S(2)}) copy-start(bf16[128,5120]{1,0:T(8,128)(2,1)} %param.18) | copy-start | bytes 3932164
  23.7 7.2 %copy-start.3 = (f32[256,256]{1,0:T(8,128)}, f32[256,256]{1,0:T(8,128)S(1)}, u32[]{:S(2)}) copy-start(f32[256,256]{1,0:T(8,128)S(1)} %fusion.148) | copy-start | bytes 786436
  23.7 1.7 copy-start.13
  25.4 1.2 copy-start.8
  138.0 2.5 copy-start.4
  139.1 1.3 copy-start.10
  139.1 2.5 copy-start.15
  139.4 0.8 copy-start.1
  139.4 3.2 %copy-start.12 = (bf16[320,128]{1,0:T(8,128)(2,1)S(1)}, bf16[320,128]{1,0:T(8,128)(2,1)}, u32[]{:S(2)}) copy-start(bf16[320,128]{1,0:T(8,128)(2,1)} %convolution_convert_fusion.4) | copy-start | bytes 245764
  141.9 0.7 copy-start.7
  143.7 10.8 %all-to-all-start = ((bf16[2,160,512]{2,0,1:T(2,128)(2,1)}), bf16[2,160,512]{2,0,1:T(2,128)(2,1)}, u32[]{:S(2)}, u32[]{:S(2)}) async-start(bf16[2,160,512]{2,0,1:T(2,128)(2,1)} %copy.12), calls=%async_computation | async-start | bytes 655360 | tf_op jit(solution)/shard_map/all_to_all | solution.py:118
  148.2 160.7 %all-reduce.9.cloned.1.call-start = ((), (), s32[]{:S(2)}) async-start(), calls=%async_computation.4 | async-start | bytes 196608 | tf_op jit(solution)/shard_map/psum | solution.py:143
  158.0 2.5 copy-start.9
  180.6 2.4 copy-start.2
  180.6 2.4 copy-start.11
  183.3 1.9 slice-start
Sparse Core Ops, SparseCore 0:
  20.2 92.6 all-reduce.4
  115.1 22.7 all-reduce.6
  185.3 123.5 all-reduce.8
